TPU v7x, 256 devices: a whole 4x4x8 slice. The times are simulated.
256 devices in a mesh: tm: 16 (over x_hi, z), tensor: 16 (over x_lo, y, core).
Axes of the slice: x: 4 (x_hi: 2, x_lo: 2; x = x_hi * 2 + x_lo), y: 4, z: 8, core: 2. Of those that a mesh axis runs over, the one named last changes fastest.
Arguments:
- features: bfloat16 [2, 2048, 1536], P(None, 'tm'), may hold values from -6 to 6
- lengths: int32 [2], replicated, may hold values from 512 to 2048, as said below
- norm_gains: float32 [2, 1536], replicated, may hold values from 0.1 to 1.9
- qkv_weight: bfloat16 [3, 1536, 1536], P(None, 'tensor'), may hold values from -0.21650635 to 0.21650635
- pos_weight: bfloat16 [1536, 1536], P('tensor'), may hold values from -0.15625 to 0.15625
- pos_biases: float32 [2, 1536], P(None, 'tensor'), may hold values from -3 to 3
- out_weight: bfloat16 [1536, 1536], P('tensor'), may hold values from -0.15625 to 0.15625
- conv_in_weight: bfloat16 [2, 1536, 1536], P(None, 'tensor'), may hold values from -0.15625 to 0.15625
- depth_kernel: float32 [31, 1536], P(None, 'tensor'), may hold values from -1 to 1
- conv_scale: float32 [1536], P('tensor'), may hold values from 0.1 to 1.9
- conv_shift: float32 [1536], P('tensor'), may hold values from -3 to 3
- conv_out_weight: bfloat16 [1536, 1536], P('tensor'), may hold values from -0.15625 to 0.15625
Outputs:
- encoded: bfloat16 [2, 2048, 1536], P(None, ('tm', 'tensor'))
Inputs may be any that keep to these rules, and one draw needn't show every extreme that they name: `lengths`: the first window is whole.
All inputs are finite; a program needn't handle non-finite values.
Results may differ from a plain program's by a relative error of at most 0.017.
Values may be sent and summed in bfloat16 or wider, within the bound.
A program may use at most 64 MiB of HBM per device.

v0:
```python
import math

import jax
import jax.numpy as jnp
from jax import lax
from jax.sharding import PartitionSpec as P

HD = 96


epsilon = 1e-05


def padded_2(cells, sides, width):
    for axis, dim in sides:
        count = lax.axis_size(axis)
        ends = count - 1
        head = lax.slice_in_dim(cells, 0, width, axis=dim)
        tail = lax.slice_in_dim(cells, cells.shape[dim] - width, cells.shape[dim], axis=dim)
        cells = jnp.concatenate(
            [
                lax.ppermute(tail, axis, [(i, (i + 1) % count) for i in range(ends)]),
                cells,
                lax.ppermute(head, axis, [((i + 1) % count, i) for i in range(ends)]),
            ],
            axis=dim,
        )
    return cells


def layer_norm(values, gain):
    values = values.astype(jnp.float32)
    row_mean = jnp.mean(values, axis=-1, keepdims=True)
    centred = values - row_mean
    variance = jnp.mean(centred * centred, axis=-1, keepdims=True)
    return centred * lax.rsqrt(variance + epsilon) * gain


def positions(offsets, model_width, pos_weight):
    half_width = model_width // 2
    frequency = jnp.exp(
        jnp.arange(half_width, dtype=jnp.float32) * (-2.0 * math.log(10000.0) / model_width)
    )
    angles = offsets.astype(jnp.float32)[:, None] * frequency[None, :]
    pos_table = jnp.concatenate(
        [jnp.sin(angles).astype(jnp.bfloat16), jnp.cos(angles).astype(jnp.bfloat16)], axis=1
    )
    return jnp.einsum(
        "md,cd->mc", pos_table, pos_weight, preferred_element_type=jnp.float32
    ).astype(jnp.bfloat16)


def diagonal_take(pos_table, row_count, col_count):
    table_width = pos_table.shape[-1]
    leading = pos_table.shape[:-2]
    flattened = pos_table.reshape(leading + (row_count * table_width,))
    flattened = lax.slice_in_dim(
        flattened,
        row_count - 1,
        row_count - 1 + row_count * (table_width - 1),
        axis=flattened.ndim - 1,
    )
    return flattened.reshape(leading + (row_count, table_width - 1))[..., :col_count]


def shards(
    features,
    lengths,
    norm_gains,
    qkv_weight,
    pos_weight,
    pos_biases,
    out_weight,
    conv_in_weight,
    depth_kernel,
    conv_scale,
    conv_shift,
    conv_out_weight,
):
    windows, local_rows, model_width = features.shape
    channels = qkv_weight.shape[1]
    heads_here = channels // HD
    score_scale = 1.0 / math.sqrt(HD)
    first_frame = lax.axis_index("tm") * local_rows
    frame_ids = first_frame + jnp.arange(local_rows, dtype=jnp.int32)
    normed = layer_norm(features, norm_gains[0]).astype(jnp.bfloat16)
    projections = jnp.einsum(
        "btd,gcd->btgc", normed, qkv_weight, preferred_element_type=jnp.float32
    )
    query_all = projections[:, :, 0]
    content_q = (
        (query_all + pos_biases[0])
        .astype(jnp.bfloat16)
        .reshape(windows, local_rows, heads_here, HD)
    )
    position_q = (
        (query_all + pos_biases[1])
        .astype(jnp.bfloat16)
        .reshape(windows, local_rows, heads_here, HD)
    )
    key_rows = projections[:, :, 1].astype(jnp.bfloat16)
    value_rows = projections[:, :, 2].astype(jnp.bfloat16)
    global_frames = local_rows * lax.axis_size("tm")
    table_rows = global_frames + local_rows - 1
    all_offsets = first_frame + local_rows - 1 - jnp.arange(table_rows, dtype=jnp.int32)
    relative_all = positions(all_offsets, model_width, pos_weight).reshape(
        table_rows, heads_here, HD
    )
    running_max = jnp.full((windows, heads_here, local_rows), -1e30, jnp.float32)
    key_piece = lax.all_gather(key_rows, "tm", axis=1, tiled=True)
    value_piece = lax.all_gather(value_rows, "tm", axis=1, tiled=True)
    key_count = key_piece.shape[1]
    key_heads = key_piece.reshape(windows, key_count, heads_here, HD)
    value_heads = value_piece.reshape(windows, key_count, heads_here, HD)
    content_scores = jnp.einsum(
        "bqhe,bkhe->bhqk", content_q, key_heads, preferred_element_type=jnp.float32
    )
    full_pos = jnp.einsum(
        "bqhe,mhe->bhqm", position_q, relative_all, preferred_element_type=jnp.float32
    )
    scores = (content_scores + diagonal_take(full_pos, local_rows, key_count)) * score_scale
    key_ids = jnp.arange(key_count, dtype=jnp.int32)
    key_mask = (key_ids[None, :] < lengths[:, None])[:, None, None, :]
    scores = jnp.where(key_mask, scores, -1e30)
    new_max = jnp.maximum(running_max, jnp.max(scores, axis=-1))
    attention_weights = jnp.where(key_mask, jnp.exp(scores - new_max[..., None]), 0.0)
    running_sum = jnp.sum(attention_weights, axis=-1)
    weighted = jnp.einsum(
        "bhqk,bkhe->bhqe",
        attention_weights.astype(jnp.bfloat16),
        value_heads,
        preferred_element_type=jnp.float32,
    )
    head_outputs = (weighted / running_sum[..., None]).astype(jnp.bfloat16)
    head_outputs = head_outputs.transpose(0, 2, 1, 3).reshape(windows, local_rows, channels)
    attention_term = jnp.einsum(
        "btc,cd->btd", head_outputs, out_weight, preferred_element_type=jnp.float32
    )
    row_count = local_rows // lax.axis_size("tensor")
    row_start = lax.axis_index("tensor") * row_count
    attention_full = lax.psum(attention_term.astype(jnp.bfloat16), "tensor").astype(jnp.float32)
    hidden = (features.astype(jnp.float32) + attention_full).astype(jnp.bfloat16)
    hidden_rows = lax.dynamic_slice_in_dim(hidden, row_start, row_count, 1)
    normed_two = layer_norm(hidden, norm_gains[1]).astype(jnp.bfloat16)
    widened = jnp.einsum(
        "btd,gcd->btgc", normed_two, conv_in_weight, preferred_element_type=jnp.float32
    )
    gated_units = widened[:, :, 0] * jax.nn.sigmoid(widened[:, :, 1])
    frame_valid = frame_ids[None, :] < lengths[:, None]
    gated_units = jnp.where(frame_valid[:, :, None], gated_units, 0.0).astype(jnp.bfloat16)
    rim = depth_kernel.shape[0] // 2
    padded = padded_2(gated_units, (("tm", 1),), rim)
    depth_sum = jnp.zeros(gated_units.shape, jnp.float32)
    for tap_index in range(depth_kernel.shape[0]):
        depth_sum = (
            depth_sum
            + padded[:, tap_index : tap_index + local_rows].astype(jnp.float32)
            * depth_kernel[tap_index]
        )
    affine = depth_sum * conv_scale + conv_shift
    activated = (affine * jax.nn.sigmoid(affine)).astype(jnp.bfloat16)
    conv_term = jnp.einsum(
        "btc,cd->btd", activated, conv_out_weight, preferred_element_type=jnp.float32
    )
    conv_rows = lax.psum_scatter(
        conv_term.astype(jnp.bfloat16), "tensor", scatter_dimension=1, tiled=True
    ).astype(jnp.float32)
    return (hidden_rows.astype(jnp.float32) + conv_rows).astype(jnp.bfloat16)


def solution(mesh):
    return jax.shard_map(
        shards,
        mesh=mesh,
        in_specs=(
            P(None, "tm", None),
            P(),
            P(),
            P(None, "tensor", None),
            P("tensor", None),
            P(None, "tensor"),
            P("tensor", None),
            P(None, "tensor", None),
            P(None, "tensor"),
            P("tensor"),
            P("tensor"),
            P("tensor", None),
        ),
        out_specs=P(None, ("tm", "tensor"), None),
        check_vma=False,
    )
```

profile of v0, /device:TPU:1, one launch (start us, length us, event | category | flops | bytes accessed | tf_op | source)
XLA Modules:
  0.0 362.1 jit_solution(17981048727000011265)
XLA Ops:
  6.5 0.0 copy-start
  6.5 0.0 all-reduce.2.cloned.1.call-start
  6.5 0.8 slice_reduce_fusion
  7.4 1.3 convert_reduce_fusion
  8.7 1.5 fusion.21
  10.2 0.8 slice_bitcast_fusion.32
  11.0 26.0 %fusion = (bf16[2175,768]{1,0:T(8,128)(2,1)}, bf16[2175,768]{1,0:T(8,128)(2,1)}) fusion(f32[768]{0:T(1024)S(1)} %multiply_exponential_fusion, f32[2175]{0:T(1024)S(1)} %subtract_convert_fusion), kind=kLoop, calls=%fused_computation.2 | loop fusion | flops 5011200 | bytes 6693372 | tf_op jit(solution)/shard_map/convert_element_type | solution.py:46
  37.0 0.0 copy-done
  37.0 0.0 copy-done.1
  37.0 0.5 fusion.171
  37.6 0.7 copy-done.3
  38.3 6.8 %convolution_bitcast_fusion = f32[2,1,128,2175]{2,3,0,1:T(8,128)} fusion(bf16[96,1536]{1,0:T(8,128)(2,1)S(1)} %copy-done.7, bf16[2175,768]{1,0:T(8,128)(2,1)} %get-tuple-element.45, bf16[2175,768]{1,0:T(8,128)(2,1)} %get-tuple-element.44, f32[2,128,3,96]{1,3,2,0:T(8,128)S(1)} %get-tuple-element.49, f32[96]{0:T(128)S(1)} %get-tuple-element.47), kind=kOutput, calls=%fused_computation.8 | convolution fusion | flops 761960320 | bytes 9302528 | tf_op jit(solution)/shard_map/bqhe,mhe->bhqm/dot_general | solution.py:118
  45.1 2.0 copy.14
  47.1 4.4 %reshape.176 = f32[2,1,278400]{2,0,1:T(2,128)} reshape(f32[2,1,128,2175]{3,2,0,1:T(8,128)S(1)} %copy.14) | data formatting | bytes 4454400 | tf_op jit(solution)/shard_map/reshape | solution.py:56
  51.5 3.9 %slice.330 = f32[2,1,278272]{2,0,1:T(2,128)S(1)} slice(f32[2,1,278400]{2,0,1:T(2,128)} %reshape.176), slice={[0:2], [0:1], [127:278399]} | slice | bytes 4452352 | tf_op jit(solution)/shard_map/slice | solution.py:57
  55.4 0.0 copy-start.5
  55.5 4.5 %reshape.177 = f32[2,1,128,2174]{3,2,0,1:T(8,128)} reshape(f32[2,1,278272]{2,0,1:T(2,128)S(1)} %slice.330) | data formatting | bytes 4452352 | tf_op jit(solution)/shard_map/reshape | solution.py:63
  59.9 42.0 %all-gather = bf16[2,2048,1,96]{1,3,2,0:T(8,128)(2,1)S(1)} all-gather(bf16[2,128,1,96]{1,3,2,0:T(8,128)(2,1)S(1)} %get-tuple-element.10), channel_id=2, replica_groups=mesh['tm'=16,'tensor'=16] {'tm'}, dimensions={1}, use_global_device_ids=true | all-gather | bytes 835584 | tf_op jit(solution)/shard_map/all_gather | solution.py:110
  101.9 0.1 iota_compare_fusion
  102.0 2.4 fusion.172
  104.4 0.0 copy-start.2
  104.4 35.9 %all-gather.1 = bf16[2,2048,1,96]{1,3,2,0:T(8,128)(2,1)} all-gather(bf16[2,128,1,96]{1,3,2,0:T(8,128)(2,1)S(1)} %get-tuple-element.9), channel_id=3, replica_groups=mesh['tm'=16,'tensor'=16] {'tm'}, dimensions={1}, use_global_device_ids=true | all-gather | bytes 835584 | tf_op jit(solution)/shard_map/all_gather | solution.py:111
  140.3 0.5 fusion.19
  140.8 0.0 copy-start.4
  140.9 2.9 convolution_convert_fusion.1
  143.7 0.0 all-reduce.2.cloned.1.call-update
  143.8 0.0 reduce-scatter.4.cloned.1.call-start
  143.8 0.1 broadcast_compare_fusion
  143.9 133.6 %all-reduce.2.cloned.1.call-done = bf16[2,128,1536]{2,1,0:T(8,128)(2,1)} async-done(((bf16[2,128,1536]{2,1,0:T(8,128)(2,1)}), bf16[2,128,1536]{2,1,0:T(8,128)(2,1)}) %all-reduce.2.cloned.1.call-update) | async-done | bytes 786448 | tf_op jit(solution)/shard_map/psum | solution.py:141
  277.5 1.7 convert_reduce_fusion.1
  279.2 0.0 copy-start.9
  279.2 0.0 copy-start.10
  279.2 0.3 fusion.24
  279.6 0.5 fusion.49
  280.2 0.1 fusion.170
  280.3 3.2 collective-permute-start
  283.4 1.3 collective-permute-start.1
  284.8 0.0 collective-permute-done
  284.8 3.5 collective-permute-done.1
  288.3 0.0 copy-done.8
  288.3 0.0 copy-done.10
  288.3 1.7 convolution_convert_fusion
  290.0 0.8 copy.17
  290.8 1.0 copy.19
  291.8 0.0 reduce-scatter.4.cloned.1.call-update
  291.8 62.0 %reduce-scatter.4.cloned.1.call-done = bf16[8,3072]{1,0:T(8,128)(2,1)} async-done(((bf16[128,3072]{1,0:T(8,128)(2,1)}), bf16[8,3072]{1,0:T(8,128)(2,1)}) %reduce-scatter.4.cloned.1.call-update) | async-done | bytes 49168
  353.8 0.8 reshape.190
  354.6 0.6 add_convert_fusion
  (23 shorter events, 0.1 us)
Async XLA Ops:
  6.5 30.5 %copy-start = (bf16[3,96,1536]{2,1,0:T(8,128)(2,1)S(1)}, bf16[3,96,1536]{2,1,0:T(8,128)(2,1)}, u32[]{:S(2)}) copy-start(bf16[3,96,1536]{2,1,0:T(8,128)(2,1)} %param.15) | copy-start | bytes 2654212
  6.5 271.0 %all-reduce.2.cloned.1.call-start = ((), (), s32[]{:S(2)}) async-start(), calls=%async_computation.1 | async-start | bytes 1572864 | tf_op jit(solution)/shard_map/psum | solution.py:141
  11.0 26.0 %copy-start.1 = (bf16[2,128,1536]{2,1,0:T(8,128)(2,1)S(1)}, bf16[2,128,1536]{2,1,0:T(8,128)(2,1)}, u32[]{:S(2)}) copy-start(bf16[2,128,1536]{2,1,0:T(8,128)(2,1)} %param.12) | copy-start | bytes 2359300
  37.0 1.3 copy-start.7
  37.6 0.7 copy-start.3
  55.4 46.5 %copy-start.5 = (s32[2]{0:T(128)S(1)}, s32[2]{0:T(128)}, u32[]{:S(2)}) copy-start(s32[2]{0:T(128)} %param.13) | copy-start | bytes 28
  104.4 36.5 %copy-start.2 = (bf16[96,1536]{1,0:T(8,128)(2,1)S(1)}, bf16[96,1536]{1,0:T(8,128)(2,1)}, u32[]{:S(2)}) copy-start(bf16[96,1536]{1,0:T(8,128)(2,1)} %param.18) | copy-start | bytes 884740
  140.8 3.1 copy-start.4
  143.7 135.8 %copy-start.6 = (bf16[2,96,1536]{2,1,0:T(8,128)(2,1)S(1)}, bf16[2,96,1536]{2,1,0:T(8,128)(2,1)}, u32[]{:S(2)}) copy-start(bf16[2,96,1536]{2,1,0:T(8,128)(2,1)} %param.19) | copy-start | bytes 1769476
  143.8 210.1 %reduce-scatter.4.cloned.1.call-start = ((), (), s32[]{:S(2)}) async-start(), calls=%async_computation.2 | async-start | bytes 835584
  279.2 9.1 %copy-start.8 = (bf16[96,1536]{1,0:T(8,128)(2,1)S(1)}, bf16[96,1536]{1,0:T(8,128)(2,1)}, u32[]{:S(2)}) copy-start(bf16[96,1536]{1,0:T(8,128)(2,1)} %param.23) | copy-start | bytes 884740
  279.2 9.1 %copy-start.9 = (f32[96]{0:T(128)S(1)}, f32[96]{0:T(128)}, u32[]{:S(2)}) copy-start(f32[96]{0:T(128)} %param.22) | copy-start | bytes 1156
  279.2 9.1 %copy-start.10 = (f32[96]{0:T(128)S(1)}, f32[96]{0:T(128)}, u32[]{:S(2)}) copy-start(f32[96]{0:T(128)} %param.21) | copy-start | bytes 1156
  280.3 4.5 %collective-permute-start = (bf16[2,15,96]{1,2,0:T(8,128)(2,1)S(1)}, bf16[2,15,96]{1,2,0:T(8,128)(2,1)S(1)}, u32[]{:S(2)}, u32[]{:S(2)}) collective-permute-start(bf16[2,15,96]{1,2,0:T(8,128)(2,1)S(1)} %get-tuple-element.11), channel_id=1, source_target_pairs={{0,16},{16,32},{32,48},{48,64},{64,80},{80,96},{96,112},{112,128},... | collective-permute-start | bytes 17288 | tf_op jit(solution)/shard_map/ppermute | solution.py:22
  283.4 4.8 %collective-permute-start.1 = (bf16[2,15,96]{1,2,0:T(8,128)(2,1)S(1)}, bf16[2,15,96]{1,2,0:T(8,128)(2,1)S(1)}, u32[]{:S(2)}, u32[]{:S(2)}) collective-permute-start(bf16[2,15,96]{1,2,0:T(8,128)(2,1)S(1)} %get-tuple-element.12), channel_id=1, source_target_pairs={{16,0},{32,16},{48,32},{64,48},{80,64},{96,80},{112,96},{128,112},... | collective-permute-start | bytes 17288 | tf_op jit(solution)/shard_map/ppermute | solution.py:24
Sparse Core Ops, SparseCore 0:
  143.9 133.5 all-reduce.1
  291.9 61.8 reduce-scatter.3
where the time goes:
time: 365 us; the launch traced here: 362 us
  waiting for transfers between devices  199 us (55%)
  blocking collectives  77.9 us (21%)
  other arithmetic  32.2 us (9%)
  local copies, waits for them, and re-layouts  19.9 us (5%)
  matrix products  14.8 us (4%)
  between operations  13.7 us (4%)
  starting transfers between devices  4.51 us (1%)
    psum x1, waiting for transfers between devices, shards(): lax.psum(attention_term.astype(jnp.bfloat16), 'tensor').astype(jnp.float32)  134 us
    unnamed x3, waiting for transfers between devices  62 us
    all_gather x1, blocking collectives, shards(): key_piece = lax.all_gather(key_rows, 'tm', axis=1, tiled=True)  42 us
    all_gather x1, blocking collectives, shards(): value_piece = lax.all_gather(value_rows, 'tm', axis=1, tiled=True)  35.9 us
    convert_element_type x1, other arithmetic, positions(): jnp.sin(angles).astype(jnp.bfloat16)  26 us
  transfers between devices with their start and end apart: 4, of which 3 were waited for; matrix products, arithmetic and copies ran while one was open for 0% of the time, Pallas kernels for 0%

commit v1 on v0

v1 whole, which is shorter than its diff:
```python
import math

import jax
import jax.numpy as jnp
from jax import lax
from jax.experimental import pallas as pl
from jax.experimental.pallas import tpu as pltpu
from jax.sharding import PartitionSpec as P

MESH = pl.DeviceIdType.MESH
HD = 96
D = 1536
HALF = D // 2
TILE = 128
EPS = 1e-05
F32 = jnp.float32
BF16 = jnp.bfloat16


def layer_norm(values, gain):
    row_mean = jnp.mean(values, axis=-1, keepdims=True)
    centred = values - row_mean
    variance = jnp.mean(centred * centred, axis=-1, keepdims=True)
    return centred * lax.rsqrt(variance + EPS) * gain


def dot_nt(a, b):
    return lax.dot_general(a, b, (((1,), (1,)), ((), ())), preferred_element_type=F32)


def dot_nn(a, b):
    return jnp.dot(a, b, preferred_element_type=F32)


def rcopy(src, dst, send_sem, recv_sem, tm, tensor):
    return pltpu.make_async_remote_copy(
        src_ref=src,
        dst_ref=dst,
        send_sem=send_sem,
        recv_sem=recv_sem,
        device_id=(tm, tensor),
        device_id_type=MESH,
    )


def bulk_wait(ref, sem):
    pltpu.make_async_copy(ref, ref, sem).wait()


def kernel(
    lens,
    feat,
    gains,
    wqkv,
    wpos,
    pbias,
    wout,
    wcin,
    dker,
    cscale,
    cshift,
    wcout,
    out,
    xs,
    normed,
    kv,
    q_content,
    q_position,
    fine_sin,
    fine_cos,
    coarse_sin,
    coarse_cos,
    rot,
    scores,
    wo,
    wc,
    hsend,
    hrecv,
    asend,
    arecv,
    nbuf,
    gbuf,
    kv_send,
    ring_recv,
    cross_recv,
    w_send,
    wy_recv,
    wx_recv,
    ws_recv,
    w_local,
    a2a_send,
    a2a_recv,
    n_send,
    n_recv,
    ns_recv,
    halo_send,
    halo_recv,
):
    t = lax.axis_index("tm")
    s = lax.axis_index("tensor")
    z = t % 8
    base = (t // 8) * 8
    other = 8 - base
    z_right = base + (z + 1) % 8
    z_left = base + (z + 7) % 8
    t_cross = (t + 8) % 16
    core = s % 2
    y = (s // 2) % 4
    x_base = (s // 8) * 8
    sibling = s + 1 - 2 * core
    s_cross = (s + 8) % 16
    score_scale = 1.0 / math.sqrt(HD)

    barrier = pltpu.get_barrier_semaphore()
    peers = [(t, (s + k) % 16) for k in range(1, 16)]
    peers += [(t_cross, s_cross), (t_cross, s), (z_right, s), (z_left, s)]
    peers += [((t + 1) % 16, s), ((t + 15) % 16, s)]
    for peer in peers:
        pl.semaphore_signal(barrier, inc=1, device_id=peer, device_id_type=MESH)

    gain_one = gains[0:1, :]
    for w in range(2):

        @pl.loop(0, 8)
        def _(i, w=w):
            rows = feat[w, pl.ds(pl.multiple_of(i * 16, 16), 16), :].astype(F32)
            xs[w, pl.ds(i * 2, 2)] = rows.reshape(2, 8, D)
            normed[pl.ds(pl.multiple_of(w * TILE + i * 16, 16), 16), :] = layer_norm(
                rows, gain_one
            ).astype(BF16)

    kv[t] = dot_nt(wqkv[1:3].reshape(2 * HD, D), normed[...]).astype(BF16)

    pl.semaphore_wait(barrier, len(peers))

    def block(column, offset):
        return (base if column == 0 else other) + (z + offset) % 8

    def part(v, way, d):
        return kv.at[v] if d < 3 else kv.at[v, pl.ds(HD * way, HD)]

    def ring_send(column, d):
        for way in range(2):
            ref = part(block(column, 8 - d if way == 0 else d), way, d)
            rcopy(
                ref,
                ref,
                kv_send,
                ring_recv.at[way, column, d],
                z_right if way == 0 else z_left,
                s,
            ).start()

    def ring_wait(column, d):
        for way in range(2):
            ref = part(block(column, 7 - d if way == 0 else d + 1), way, d)
            rcopy(
                ref,
                ref,
                kv_send,
                ring_recv.at[way, column, d],
                z_right if way == 0 else z_left,
                s,
            ).wait_recv()

    def y_peer(k):
        return x_base + ((y + k) % 4) * 2 + core

    def weights_start(i, own, buf):
        for k in (1, 3, 2):
            rcopy(own, buf.at[s], w_send.at[i], wy_recv.at[i, 4 - k], t, y_peer(k)).start()
        for half, tm in ((0, t), (1, t_cross)):
            rows = pl.ds(48 * half, 48)
            rcopy(
                own.at[rows], buf.at[s, rows], w_send.at[i], wx_recv.at[i, 0], tm, s_cross
            ).start()
        rcopy(own, buf.at[s], w_send.at[i], ws_recv.at[i], t, sibling).start()
        pltpu.make_async_copy(own, buf.at[s], w_local.at[i]).start()

    def weights_y(i, own, buf, k):
        p = y_peer(k)
        rcopy(own, buf.at[p], w_send.at[i], wy_recv.at[i, k], t, y_peer(k)).wait_recv()
        for half, tm in ((0, t), (1, t_cross)):
            ref = buf.at[p, pl.ds(48 * half, 48)]
            rcopy(ref, ref, w_send.at[i], wx_recv.at[i, k], tm, s_cross).start()
        rcopy(buf.at[p], buf.at[p], w_send.at[i], ws_recv.at[i], t, sibling).start()

    def weights_x(i, buf, k):
        p = (y_peer(k) + 8) % 16
        bulk_wait(buf.at[p], wx_recv.at[i, k])
        rcopy(buf.at[p], buf.at[p], w_send.at[i], ws_recv.at[i], t, sibling).start()

    def weights_end(i, own, buf):
        bulk_wait(buf.at[pl.ds(0, 8)], ws_recv.at[i])
        pltpu.make_async_copy(own, buf.at[s], w_local.at[i]).wait()

    ring_send(0, 0)
    rcopy(kv.at[t], kv.at[t], kv_send, cross_recv, t_cross, s).start()
    weights_start(0, wout, wo)

    query = dot_nt(normed[...], wqkv[0])
    q_content[...] = (query + pbias[0:1, :]).astype(BF16)
    q_position[...] = (query + pbias[1:2, :]).astype(BF16)
    frequency = jnp.exp(
        lax.broadcasted_iota(jnp.int32, (1, HALF), 1).astype(F32)
        * (-2.0 * math.log(10000.0) / D)
    )

    n_ids = lax.broadcasted_iota(jnp.int32, (24, 1), 0)
    coarse = ((t - n_ids) * TILE).astype(F32) * frequency
    coarse_sin[...] = jnp.sin(coarse)
    coarse_cos[...] = jnp.cos(coarse)

    @pl.loop(0, 8)
    def _(i):
        ids = 127 - i * 16 - lax.broadcasted_iota(jnp.int32, (16, 1), 0)
        angle = ids.astype(F32) * frequency
        rows = pl.ds(pl.multiple_of(i * 16, 16), 16)
        fine_sin[rows, :] = jnp.sin(angle)
        fine_cos[rows, :] = jnp.cos(angle)

    def rel_tiles(start, stop):
        @pl.loop(start, stop)
        def _(n):
            a_sin = coarse_sin[pl.ds(n, 1), :]
            a_cos = coarse_cos[pl.ds(n, 1), :]
            f_sin = fine_sin[...]
            f_cos = fine_cos[...]
            pe_sin = (a_sin * f_cos + a_cos * f_sin).astype(BF16)
            pe_cos = (a_cos * f_cos - a_sin * f_sin).astype(BF16)
            rel = dot_nt(wpos[:, 0:HALF], pe_sin) + dot_nt(wpos[:, HALF:D], pe_cos)
            part_scores = dot_nn(q_position[...], rel.astype(BF16))
            for w in range(2):
                rot[n, pl.ds(w * TILE, TILE), :] = pltpu.roll(
                    part_scores[w * TILE : (w + 1) * TILE],
                    1,
                    1,
                    stride=1,
                    stride_axis=0,
                )

    row_ids = lax.broadcasted_iota(jnp.int32, (TILE, TILE), 0)
    col_ids = lax.broadcasted_iota(jnp.int32, (TILE, TILE), 1)

    def content(v):
        for w in range(2):
            rows = pl.ds(w * TILE, TILE)
            value = dot_nn(q_content[rows, :], kv[v, 0:HD, pl.ds(w * TILE, TILE)])
            value = value + jnp.where(col_ids <= row_ids, rot[v, rows, :], rot[v + 1, rows, :])
            valid = v * TILE + col_ids < lens[w]
            scores[v, rows, :] = jnp.where(valid, value * score_scale, -1e30)

    def content_pair(column, d):
        content(block(column, 7 - d))
        content(block(column, d + 1))

    ring_wait(0, 0)
    ring_send(0, 1)
    rel_tiles(0, 4)
    rcopy(kv.at[t_cross], kv.at[t_cross], kv_send, cross_recv, t_cross, s).wait_recv()
    ring_send(1, 0)
    rel_tiles(4, 8)
    ring_wait(0, 1)
    ring_send(0, 2)
    rel_tiles(8, 12)
    ring_wait(1, 0)
    ring_send(1, 1)
    weights_y(0, wout, wo, 1)
    weights_y(0, wout, wo, 3)
    rel_tiles(12, 17)
    ring_wait(0, 2)
    ring_send(0, 3)
    content(t)
    content(t_cross)
    content_pair(0, 0)
    weights_x(0, wo, 0)
    ring_wait(1, 1)
    ring_send(1, 2)
    weights_y(0, wout, wo, 2)
    content_pair(1, 0)
    content_pair(0, 1)
    ring_wait(1, 2)
    ring_send(1, 3)
    ring_wait(0, 3)
    content_pair(0, 2)
    content_pair(1, 1)
    content(block(0, 4))
    weights_x(0, wo, 1)
    weights_x(0, wo, 3)
    content_pair(1, 2)
    ring_wait(1, 3)
    content(block(1, 4))
    weights_x(0, wo, 2)
    weights_start(1, wcout, wc)

    peak = jnp.max(scores[...], axis=0)
    peak = jnp.max(peak, axis=-1, keepdims=True)
    gathered = [jnp.zeros((TILE, HD), F32) for _ in range(2)]
    totals = [jnp.zeros((TILE, TILE), F32) for _ in range(2)]
    for v in range(16):
        for w in range(2):
            rows = slice(w * TILE, (w + 1) * TILE)
            weight = jnp.exp(scores[v, rows, :] - peak[rows])
            weight = jnp.where(v * TILE + col_ids < lens[w], weight, 0.0)
            totals[w] = totals[w] + weight
            gathered[w] = gathered[w] + dot_nt(
                weight.astype(BF16), kv[v, HD : 2 * HD, rows]
            )
    heads = [
        (gathered[w] / jnp.sum(totals[w], axis=-1, keepdims=True)).reshape(16, 8, HD)
        for w in range(2)
    ]

    def exchange(i, send, recv, cells):
        send[:, :, 0:HD] = jnp.concatenate(cells, axis=1).astype(BF16)
        for k in range(1, 16):
            p = (s + k) % 16
            rcopy(send.at[p], recv.at[s], a2a_send.at[i], a2a_recv.at[i], t, p).start()
        own = pltpu.make_async_copy(send.at[s], recv.at[s], a2a_recv.at[i])
        own.start()
        bulk_wait(recv, a2a_recv.at[i])

    exchange(0, hsend, hrecv, heads)
    weights_end(0, wout, wo)
    total = dot_nn(hrecv[0, :, 0:HD], wo[0])
    for k in range(1, 16):
        total = total + dot_nn(hrecv[k, :, 0:HD], wo[k])
    own_rows = jnp.concatenate([xs[0, s], xs[1, s]], axis=0)
    hidden = (own_rows + total).astype(BF16).astype(F32)
    nbuf[s] = layer_norm(hidden, gains[1:2, :]).astype(BF16)

    steps = [(1, 0), (0, 1), (0, 3), (1, 1), (1, 3), (0, 2), (1, 2)]

    def n_peer(dx, dy):
        return (x_base + 8 * dx) % 16 + ((y + dy) % 4) * 2 + core

    for j, (dx, dy) in enumerate(steps):
        rcopy(
            nbuf.at[s], nbuf.at[s], n_send, n_recv.at[dx * 4 + (4 - dy) % 4], t, n_peer(dx, dy)
        ).start()
    rcopy(nbuf.at[s], nbuf.at[s], n_send, ns_recv, t, sibling).start()
    for dx, dy in steps:
        p = n_peer(dx, dy)
        rcopy(nbuf.at[p], nbuf.at[p], n_send, n_recv.at[dx * 4 + dy], t, p).wait_recv()
        rcopy(nbuf.at[p], nbuf.at[p], n_send, ns_recv, t, sibling).start()
    bulk_wait(nbuf.at[pl.ds(0, 8)], ns_recv)

    rows_all = nbuf[...].reshape(256, D)
    opened = dot_nt(rows_all, wcin[0])
    gate = dot_nt(rows_all, wcin[1])
    gated = opened * jax.nn.sigmoid(gate)
    ids = lax.broadcasted_iota(jnp.int32, (256, HD), 0)
    window = (ids // 8) % 2
    frame = t * TILE + (ids // 16) * 8 + ids % 8
    limit = jnp.where(window == 0, lens[0], lens[1])
    gated = jnp.where(frame < limit, gated, 0.0).astype(BF16).astype(F32)
    gated = gated.reshape(16, 2, 8, HD)
    for w in range(2):
        gbuf[w, 16:144, 0:HD] = gated[:, w].reshape(TILE, HD)

    def halo(way):
        src = gbuf.at[:, pl.ds(16 if way == 0 else 128, 16), :]
        dst = gbuf.at[:, pl.ds(144 if way == 0 else 0, 16), :]
        tm = (t + 15) % 16 if way == 0 else (t + 1) % 16
        return rcopy(src, dst, halo_send.at[way], halo_recv.at[way], tm, s)

    halo(0).start()
    halo(1).start()
    for k in (1, 3, 2):
        weights_y(1, wcout, wc, k)
    halo(0).wait_recv()
    halo(1).wait_recv()

    @pl.when(t == 0)
    def _():
        gbuf[:, 0:16, :] = jnp.zeros((2, 16, TILE), F32)

    @pl.when(t == 15)
    def _():
        gbuf[:, 144:160, :] = jnp.zeros((2, 16, TILE), F32)

    cells = []
    for w in range(2):
        depth_sum = jnp.zeros((TILE, HD), F32)
        for k in range(31):
            depth_sum = depth_sum + gbuf[w, k + 1 : k + 1 + TILE, 0:HD] * dker[k : k + 1, :]
        affine = depth_sum * cscale[...] + cshift[...]
        cells.append((affine * jax.nn.sigmoid(affine)).reshape(16, 8, HD))

    for k in range(4):
        weights_x(1, wc, k)
    exchange(1, asend, arecv, cells)
    weights_end(1, wcout, wc)
    final = dot_nn(arecv[0, :, 0:HD], wc[0])
    for k in range(1, 16):
        final = final + dot_nn(arecv[k, :, 0:HD], wc[k])
    out[...] = (hidden + final).reshape(2, 8, D).astype(BF16)

    bulk_wait(kv.at[pl.ds(0, 15)], kv_send)
    for i, buf in ((0, wo), (1, wc)):
        bulk_wait(buf.at[pl.ds(0, 15)], w_send.at[i])
    for i, buf in ((0, hsend), (1, asend)):
        bulk_wait(buf.at[pl.ds(0, 15)], a2a_send.at[i])
    bulk_wait(nbuf.at[pl.ds(0, 15)], n_send)
    halo(0).wait_send()
    halo(1).wait_send()


def shards(
    features,
    lengths,
    norm_gains,
    qkv_weight,
    pos_weight,
    pos_biases,
    out_weight,
    conv_in_weight,
    depth_kernel,
    conv_scale,
    conv_shift,
    conv_out_weight,
):
    vmem = pl.BlockSpec(memory_space=pltpu.VMEM)
    dma = pltpu.SemaphoreType.DMA
    return pl.pallas_call(
        kernel,
        out_shape=jax.ShapeDtypeStruct((2, 8, D), BF16),
        in_specs=[pl.BlockSpec(memory_space=pltpu.SMEM)] + [vmem] * 11,
        out_specs=vmem,
        scratch_shapes=[
            pltpu.VMEM((2, 16, 8, D), F32),
            pltpu.VMEM((256, D), BF16),
            pltpu.VMEM((16, 2 * HD, 256), BF16),
            pltpu.VMEM((256, HD), BF16),
            pltpu.VMEM((256, HD), BF16),
            pltpu.VMEM((TILE, HALF), F32),
            pltpu.VMEM((TILE, HALF), F32),
            pltpu.VMEM((24, HALF), F32),
            pltpu.VMEM((24, HALF), F32),
            pltpu.VMEM((17, 256, TILE), F32),
            pltpu.VMEM((16, 256, TILE), F32),
            pltpu.VMEM((16, HD, D), BF16),
            pltpu.VMEM((16, HD, D), BF16),
            pltpu.VMEM((16, 16, TILE), BF16),
            pltpu.VMEM((16, 16, TILE), BF16),
            pltpu.VMEM((16, 16, TILE), BF16),
            pltpu.VMEM((16, 16, TILE), BF16),
            pltpu.VMEM((16, 16, D), BF16),
            pltpu.VMEM((2, 160, TILE), F32),
            dma,
            dma((2, 2, 4)),
            dma,
            dma((2,)),
            dma((2, 4)),
            dma((2, 4)),
            dma((2,)),
            dma((2,)),
            dma((2,)),
            dma((2,)),
            dma,
            dma((8,)),
            dma,
            dma((2,)),
            dma((2,)),
        ],
        compiler_params=pltpu.CompilerParams(
            collective_id=0, has_side_effects=True, vmem_limit_bytes=60 * 2**20
        ),
    )(
        lengths,
        features,
        norm_gains,
        qkv_weight,
        pos_weight,
        pos_biases,
        out_weight,
        conv_in_weight,
        depth_kernel,
        conv_scale.reshape(1, HD),
        conv_shift.reshape(1, HD),
        conv_out_weight,
    )


def solution(mesh):
    return jax.shard_map(
        shards,
        mesh=mesh,
        in_specs=(
            P(None, "tm", None),
            P(),
            P(),
            P(None, "tensor", None),
            P("tensor", None),
            P(None, "tensor"),
            P("tensor", None),
            P(None, "tensor", None),
            P(None, "tensor"),
            P("tensor"),
            P("tensor"),
            P("tensor", None),
        ),
        out_specs=P(None, ("tm", "tensor"), None),
        check_vma=False,
    )
```

time: 365 us -> 80 us (0.22)
  waiting for transfers between devices: 199 us -> 0 us
  Pallas kernels: 0 us -> 78.4 us
  blocking collectives: 77.9 us -> 0 us
  other arithmetic: 32.2 us -> 0 us
  local copies, waits for them, and re-layouts: 19.9 us -> 1.42 us
  matrix products: 14.8 us -> 0 us
  between operations: 13.7 us -> 0.01 us
  starting transfers between devices: 4.51 us -> 0 us
    psum x1 -> x0, waiting for transfers between devices: 134 us -> none  [shards(): lax.psum(attention_term.astype(jnp.bfloat16), 'tensor').astype(jnp.float32)]
    pallas_call x0 -> x1, Pallas kernels: none -> 78.4 us  [shards(): pl.pallas_call(kernel, out_shape=jax.ShapeDtypeStruct((2, 8, D), BF16), i...]
    all_gather x2 -> x0, blocking collectives: 77.9 us -> none  [the longest x1 42 us: shards(): key_piece = lax.all_gather(key_rows, 'tm', axis=1, tiled=True)]
    unnamed x3 -> x0, waiting for transfers between devices: 62 us -> none
    convert_element_type x4 -> x0, other arithmetic: 26.7 us -> none  [the longest x1 26 us: positions(): jnp.sin(angles).astype(jnp.bfloat16)]
    dot_general x6 -> x0, matrix products: 14.8 us -> none  [the longest x1 6.82 us: shards(): jnp.einsum('bqhe,mhe->bhqm', position_q, relative_all, preferred_element_...]
    reshape x2 -> x0, local copies, waits for them, and re-layouts: 8.87 us -> none  [the longest x1 4.48 us: diagonal_take(): flattened.reshape(leading + (row_count, table_width - 1))[..., :col_count]]
    reduce_sum x5 -> x0, other arithmetic: 5.34 us -> none  [the longest x2 3 us: layer_norm(): row_mean = jnp.mean(values, axis=-1, keepdims=True)]
  transfers between devices with their start and end apart: 4 -> 0, of which waited for: 3 -> 0; matrix products, arithmetic and copies ran while one was open for 0% -> 0% of each run, Pallas kernels for 0% -> 0%
where the time goes in v1:
time: 80 us; the launch traced here: 79.8 us
  Pallas kernels  78.4 us (98%)
  local copies, waits for them, and re-layouts  1.42 us (2%)
    pallas_call x1, Pallas kernels, shards(): pl.pallas_call(kernel, out_shape=jax.ShapeDtypeStruct((2, 8, D), BF16), i...  78.4 us

profile of v1, /device:TPU:1, one launch (start us, length us, event | category | flops | bytes accessed | tf_op | source)
XLA Modules:
  0.0 79.8 jit_solution(8618530564688693316)
XLA Ops:
  0.0 78.4 %shard_map.118 = bf16[2,8,1536]{2,1,0:T(8,128)(2,1)} custom-call(s32[2]{0:T(128)} %lens.1, bf16[2,128,1536]{2,1,0:T(8,128)(2,1)} %feat.1, f32[2,1536]{1,0:T(2,128)} %gains.1, bf16[3,96,1536]{2,1,0:T(8,128)(2,1)} %wqkv.1, bf16[96,1536]{1,0:T(8,128)(2,1)} %wpos.1, f32[2,96]{1,0:T(2,128)} %pbias.1, bf16[96,1536]{1,0:T(8,128)(2,1)} %wout.1, ...), custom_call_target="tpu_custom_call" | custom-call | tf_op jit(solution)/shard_map/pallas_call | solution.py:425
  78.4 1.4 %copy.14 = bf16[2,8,1536]{2,1,0:T(8,128)(2,1)} copy(bf16[2,8,1536]{2,1,0:T(8,128)(2,1)} %shard_map.118) | data formatting | bytes 98304

commit v2 on v1

--- a/solution.py
+++ b/solution.py
@@ -72,29 +72,33 @@
     coarse_cos,
     rot,
     scores,
-    wo,
-    wc,
+    wbuf,
+    params,
     hsend,
     hrecv,
-    asend,
-    arecv,
+    psend,
+    precv,
+    pown,
     nbuf,
+    gx,
     gbuf,
     kv_send,
     ring_recv,
     cross_recv,
     w_send,
-    wy_recv,
     wx_recv,
     ws_recv,
     w_local,
     a2a_send,
     a2a_recv,
+    p_send,
+    p_recv,
     n_send,
     n_recv,
-    ns_recv,
     halo_send,
     halo_recv,
+    params_send,
+    params_recv,
 ):
     t = lax.axis_index("tm")
     s = lax.axis_index("tensor")
@@ -106,17 +110,35 @@
     t_cross = (t + 8) % 16
     core = s % 2
     y = (s // 2) % 4
-    x_base = (s // 8) * 8
+    x = s // 8
+    g = x * 2 + core
     sibling = s + 1 - 2 * core
     s_cross = (s + 8) % 16
+    g_cross = (1 - x) * 2 + core
+    t_next = (t + x) % 16
+    t_prev = (t + 15 + x) % 16
+    edge = [(1 - x) * 8 + y * 2 + cc for cc in range(2)]
+
+    def y_peer(k):
+        return x * 8 + ((y + k) % 4) * 2 + core
+
+    def g_peer(k):
+        p = (g + k) % 4
+        return p, (p // 2) * 8 + y * 2 + p % 2
+
     score_scale = 1.0 / math.sqrt(HD)
 
     barrier = pltpu.get_barrier_semaphore()
-    peers = [(t, (s + k) % 16) for k in range(1, 16)]
+    peers = [(t, y_peer(k)) for k in range(1, 4)]
+    peers += [(t, g_peer(k)[1]) for k in range(1, 4)]
     peers += [(t_cross, s_cross), (t_cross, s), (z_right, s), (z_left, s)]
-    peers += [((t + 1) % 16, s), ((t + 15) % 16, s)]
+    peers += [(t_next, p) for p in edge] + [(t_prev, p) for p in edge]
     for peer in peers:
         pl.semaphore_signal(barrier, inc=1, device_id=peer, device_id_type=MESH)
+
+    params[g, 0:31, 0:HD] = dker[...]
+    params[g, 31:32, 0:HD] = cscale[...]
+    params[g, 32:33, 0:HD] = cshift[...]
 
     gain_one = gains[0:1, :]
     for w in range(2):
@@ -163,40 +185,35 @@
                 s,
             ).wait_recv()
 
-    def y_peer(k):
-        return x_base + ((y + k) % 4) * 2 + core
-
-    def weights_start(i, own, buf):
-        for k in (1, 3, 2):
-            rcopy(own, buf.at[s], w_send.at[i], wy_recv.at[i, 4 - k], t, y_peer(k)).start()
+    own_weights = [wout, wcin.at[0], wcin.at[1], wcout]
+
+    def weights_start(m):
+        own = own_weights[m]
         for half, tm in ((0, t), (1, t_cross)):
             rows = pl.ds(48 * half, 48)
             rcopy(
-                own.at[rows], buf.at[s, rows], w_send.at[i], wx_recv.at[i, 0], tm, s_cross
+                own.at[rows], wbuf.at[m, g, rows], w_send, wx_recv.at[m], tm, s_cross
             ).start()
-        rcopy(own, buf.at[s], w_send.at[i], ws_recv.at[i], t, sibling).start()
-        pltpu.make_async_copy(own, buf.at[s], w_local.at[i]).start()
-
-    def weights_y(i, own, buf, k):
-        p = y_peer(k)
-        rcopy(own, buf.at[p], w_send.at[i], wy_recv.at[i, k], t, y_peer(k)).wait_recv()
-        for half, tm in ((0, t), (1, t_cross)):
-            ref = buf.at[p, pl.ds(48 * half, 48)]
-            rcopy(ref, ref, w_send.at[i], wx_recv.at[i, k], tm, s_cross).start()
-        rcopy(buf.at[p], buf.at[p], w_send.at[i], ws_recv.at[i], t, sibling).start()
-
-    def weights_x(i, buf, k):
-        p = (y_peer(k) + 8) % 16
-        bulk_wait(buf.at[p], wx_recv.at[i, k])
-        rcopy(buf.at[p], buf.at[p], w_send.at[i], ws_recv.at[i], t, sibling).start()
-
-    def weights_end(i, own, buf):
-        bulk_wait(buf.at[pl.ds(0, 8)], ws_recv.at[i])
-        pltpu.make_async_copy(own, buf.at[s], w_local.at[i]).wait()
+        rcopy(own, wbuf.at[m, g], w_send, ws_recv.at[m], t, sibling).start()
+        pltpu.make_async_copy(own, wbuf.at[m, g], w_local.at[m]).start()
+
+    def weights_x(m):
+        ref = wbuf.at[m, g_cross]
+        bulk_wait(ref, wx_recv.at[m])
+        rcopy(ref, ref, w_send, ws_recv.at[m], t, sibling).start()
+
+    def weights_end(m):
+        bulk_wait(wbuf.at[m, pl.ds(0, 2)], ws_recv.at[m])
+        pltpu.make_async_copy(own_weights[m], wbuf.at[m, g], w_local.at[m]).wait()
 
     ring_send(0, 0)
     rcopy(kv.at[t], kv.at[t], kv_send, cross_recv, t_cross, s).start()
-    weights_start(0, wout, wo)
+    for m in range(4):
+        weights_start(m)
+    for k in range(1, 4):
+        rcopy(
+            params.at[g], params.at[g], params_send, params_recv, t, g_peer(k)[1]
+        ).start()
 
     query = dot_nt(normed[...], wqkv[0])
     q_content[...] = (query + pbias[0:1, :]).astype(BF16)
@@ -265,18 +282,15 @@
     rel_tiles(8, 12)
     ring_wait(1, 0)
     ring_send(1, 1)
-    weights_y(0, wout, wo, 1)
-    weights_y(0, wout, wo, 3)
     rel_tiles(12, 17)
     ring_wait(0, 2)
     ring_send(0, 3)
     content(t)
     content(t_cross)
     content_pair(0, 0)
-    weights_x(0, wo, 0)
+    weights_x(0)
     ring_wait(1, 1)
     ring_send(1, 2)
-    weights_y(0, wout, wo, 2)
     content_pair(1, 0)
     content_pair(0, 1)
     ring_wait(1, 2)
@@ -285,13 +299,12 @@
     content_pair(0, 2)
     content_pair(1, 1)
     content(block(0, 4))
-    weights_x(0, wo, 1)
-    weights_x(0, wo, 3)
+    weights_x(1)
     content_pair(1, 2)
     ring_wait(1, 3)
     content(block(1, 4))
-    weights_x(0, wo, 2)
-    weights_start(1, wcout, wc)
+    weights_x(2)
+    weights_x(3)
 
     peak = jnp.max(scores[...], axis=0)
     peak = jnp.max(peak, axis=-1, keepdims=True)
@@ -311,99 +324,98 @@
         for w in range(2)
     ]
 
-    def exchange(i, send, recv, cells):
-        send[:, :, 0:HD] = jnp.concatenate(cells, axis=1).astype(BF16)
-        for k in range(1, 16):
-            p = (s + k) % 16
-            rcopy(send.at[p], recv.at[s], a2a_send.at[i], a2a_recv.at[i], t, p).start()
-        own = pltpu.make_async_copy(send.at[s], recv.at[s], a2a_recv.at[i])
-        own.start()
-        bulk_wait(recv, a2a_recv.at[i])
-
-    exchange(0, hsend, hrecv, heads)
-    weights_end(0, wout, wo)
-    total = dot_nn(hrecv[0, :, 0:HD], wo[0])
-    for k in range(1, 16):
-        total = total + dot_nn(hrecv[k, :, 0:HD], wo[k])
+    cells = jnp.concatenate(heads, axis=1).astype(BF16)
+    for p in range(16):
+        hsend[(p // 8) * 2 + p % 2, (p // 2) % 4, :, 0:HD] = cells[p]
+    for k in range(1, 4):
+        p, dev = g_peer(k)
+        rcopy(hsend.at[p], hrecv.at[g], a2a_send, a2a_recv, t, dev).start()
+    pltpu.make_async_copy(hsend.at[g], hrecv.at[g], a2a_recv).start()
+    bulk_wait(hrecv, a2a_recv)
+
+    def reduce_rows(i, total):
+        total = total.reshape(4, 16, D)
+        psend[i] = total.astype(BF16)
+        for k in (2, 1, 3):
+            rcopy(
+                psend.at[i, (y + k) % 4], precv.at[i, y], p_send.at[i], p_recv.at[i], t, y_peer(k)
+            ).start()
+        pown[...] = total
+        bulk_wait(precv.at[i, pl.ds(0, 3)], p_recv.at[i])
+        result = pown[y]
+        for k in range(1, 4):
+            result = result + precv[i, (y + k) % 4].astype(F32)
+        return result
+
+    weights_end(0)
+    total = dot_nn(hrecv[0, :, :, 0:HD].reshape(64, HD), wbuf[0, 0])
+    for k in range(1, 4):
+        total = total + dot_nn(hrecv[k, :, :, 0:HD].reshape(64, HD), wbuf[0, k])
     own_rows = jnp.concatenate([xs[0, s], xs[1, s]], axis=0)
-    hidden = (own_rows + total).astype(BF16).astype(F32)
-    nbuf[s] = layer_norm(hidden, gains[1:2, :]).astype(BF16)
-
-    steps = [(1, 0), (0, 1), (0, 3), (1, 1), (1, 3), (0, 2), (1, 2)]
-
-    def n_peer(dx, dy):
-        return (x_base + 8 * dx) % 16 + ((y + dy) % 4) * 2 + core
-
-    for j, (dx, dy) in enumerate(steps):
-        rcopy(
-            nbuf.at[s], nbuf.at[s], n_send, n_recv.at[dx * 4 + (4 - dy) % 4], t, n_peer(dx, dy)
-        ).start()
-    rcopy(nbuf.at[s], nbuf.at[s], n_send, ns_recv, t, sibling).start()
-    for dx, dy in steps:
-        p = n_peer(dx, dy)
-        rcopy(nbuf.at[p], nbuf.at[p], n_send, n_recv.at[dx * 4 + dy], t, p).wait_recv()
-        rcopy(nbuf.at[p], nbuf.at[p], n_send, ns_recv, t, sibling).start()
-    bulk_wait(nbuf.at[pl.ds(0, 8)], ns_recv)
-
-    rows_all = nbuf[...].reshape(256, D)
-    opened = dot_nt(rows_all, wcin[0])
-    gate = dot_nt(rows_all, wcin[1])
+    hidden = (own_rows + reduce_rows(0, total)).astype(BF16).astype(F32)
+    nbuf[y] = layer_norm(hidden, gains[1:2, :]).astype(BF16)
+
+    for k in (2, 1, 3):
+        rcopy(nbuf.at[y], nbuf.at[y], n_send, n_recv, t, y_peer(k)).start()
+    weights_end(1)
+    weights_end(2)
+    bulk_wait(nbuf.at[pl.ds(0, 3)], n_recv)
+
+    rows_all = nbuf[...].reshape(64, D)
+    opened = dot_nt(rows_all, wbuf[1].reshape(4 * HD, D))
+    gate = dot_nt(rows_all, wbuf[2].reshape(4 * HD, D))
     gated = opened * jax.nn.sigmoid(gate)
-    ids = lax.broadcasted_iota(jnp.int32, (256, HD), 0)
+    ids = lax.broadcasted_iota(jnp.int32, (64, 4 * HD), 0)
     window = (ids // 8) % 2
-    frame = t * TILE + (ids // 16) * 8 + ids % 8
+    frame = t * TILE + x * 64 + (ids // 16) * 16 + core * 8 + ids % 8
     limit = jnp.where(window == 0, lens[0], lens[1])
-    gated = jnp.where(frame < limit, gated, 0.0).astype(BF16).astype(F32)
-    gated = gated.reshape(16, 2, 8, HD)
-    for w in range(2):
-        gbuf[w, 16:144, 0:HD] = gated[:, w].reshape(TILE, HD)
-
-    def halo(way):
-        src = gbuf.at[:, pl.ds(16 if way == 0 else 128, 16), :]
-        dst = gbuf.at[:, pl.ds(144 if way == 0 else 0, 16), :]
-        tm = (t + 15) % 16 if way == 0 else (t + 1) % 16
-        return rcopy(src, dst, halo_send.at[way], halo_recv.at[way], tm, s)
-
-    halo(0).start()
-    halo(1).start()
-    for k in (1, 3, 2):
-        weights_y(1, wcout, wc, k)
-    halo(0).wait_recv()
-    halo(1).wait_recv()
-
-    @pl.when(t == 0)
-    def _():
-        gbuf[:, 0:16, :] = jnp.zeros((2, 16, TILE), F32)
-
-    @pl.when(t == 15)
-    def _():
-        gbuf[:, 144:160, :] = jnp.zeros((2, 16, TILE), F32)
-
-    cells = []
-    for w in range(2):
-        depth_sum = jnp.zeros((TILE, HD), F32)
-        for k in range(31):
-            depth_sum = depth_sum + gbuf[w, k + 1 : k + 1 + TILE, 0:HD] * dker[k : k + 1, :]
-        affine = depth_sum * cscale[...] + cshift[...]
-        cells.append((affine * jax.nn.sigmoid(affine)).reshape(16, 8, HD))
-
-    for k in range(4):
-        weights_x(1, wc, k)
-    exchange(1, asend, arecv, cells)
-    weights_end(1, wcout, wc)
-    final = dot_nn(arecv[0, :, 0:HD], wc[0])
-    for k in range(1, 16):
-        final = final + dot_nn(arecv[k, :, 0:HD], wc[k])
+    gated = jnp.where(frame < limit, gated, 0.0).astype(BF16)
+    gx[core, 1:5] = gated.reshape(4, 16, 4 * HD)
+
+    for cc in range(2):
+        rcopy(gx.at[core, 4], gx.at[core, 0], halo_send, halo_recv, t_next, edge[cc]).start()
+        rcopy(gx.at[core, 1], gx.at[core, 5], halo_send, halo_recv, t_prev, edge[cc]).start()
+    inner = gx.at[core, pl.ds(1, 4)]
+    rcopy(inner, inner, halo_send, halo_recv, t, sibling).start()
+    bulk_wait(params.at[pl.ds(0, 3)], params_recv)
+    taps = jnp.concatenate([params[k, :, 0:HD] for k in range(4)], axis=1)
+    bulk_wait(gx.at[:, pl.ds(0, 4)], halo_recv)
+
+    first = jnp.logical_and(t == 0, x == 0)
+    last = jnp.logical_and(t == 15, x == 1)
+    for cc in range(2):
+        for j in range(6):
+            block_rows = gx[cc, j].astype(F32)
+            if j == 0:
+                block_rows = jnp.where(first, 0.0, block_rows)
+            if j == 5:
+                block_rows = jnp.where(last, 0.0, block_rows)
+            start = pl.multiple_of((2 * j + cc + 1 - core) * 8, 8)
+            for w in range(2):
+                gbuf[w, pl.ds(start, 8), :] = block_rows[w * 8 : w * 8 + 8]
+    sums = [jnp.zeros((8, 4 * HD), F32) for _ in range(8)]
+    for k in range(31):
+        tap = taps[k : k + 1, :]
+        for j in range(4):
+            for w in range(2):
+                row = 16 * j + 9 + k
+                sums[2 * j + w] = sums[2 * j + w] + gbuf[w, row : row + 8, :] * tap
+    affine = jnp.concatenate(sums, axis=0) * taps[31:32, :] + taps[32:33, :]
+    activated = (affine * jax.nn.sigmoid(affine)).astype(BF16)
+
+    weights_end(3)
+    total = dot_nn(activated, wbuf[3].reshape(4 * HD, D))
+    final = reduce_rows(1, total)
     out[...] = (hidden + final).reshape(2, 8, D).astype(BF16)
 
     bulk_wait(kv.at[pl.ds(0, 15)], kv_send)
-    for i, buf in ((0, wo), (1, wc)):
-        bulk_wait(buf.at[pl.ds(0, 15)], w_send.at[i])
-    for i, buf in ((0, hsend), (1, asend)):
-        bulk_wait(buf.at[pl.ds(0, 15)], a2a_send.at[i])
-    bulk_wait(nbuf.at[pl.ds(0, 15)], n_send)
-    halo(0).wait_send()
-    halo(1).wait_send()
+    bulk_wait(wbuf.at[pl.ds(0, 3)], w_send)
+    bulk_wait(params.at[pl.ds(0, 3)], params_send)
+    bulk_wait(hsend.at[pl.ds(0, 3)], a2a_send)
+    for i in range(2):
+        bulk_wait(psend.at[i, pl.ds(0, 3)], p_send.at[i])
+    bulk_wait(nbuf.at[pl.ds(0, 3)], n_send)
+    bulk_wait(gx.at[:, pl.ds(0, 4)], halo_send)
 
 
 def shards(
@@ -439,29 +451,33 @@
             pltpu.VMEM((24, HALF), F32),
             pltpu.VMEM((17, 256, TILE), F32),
             pltpu.VMEM((16, 256, TILE), F32),
-            pltpu.VMEM((16, HD, D), BF16),
-            pltpu.VMEM((16, HD, D), BF16),
-            pltpu.VMEM((16, 16, TILE), BF16),
-            pltpu.VMEM((16, 16, TILE), BF16),
-            pltpu.VMEM((16, 16, TILE), BF16),
-            pltpu.VMEM((16, 16, TILE), BF16),
-            pltpu.VMEM((16, 16, D), BF16),
-            pltpu.VMEM((2, 160, TILE), F32),
+            pltpu.VMEM((4, 4, HD, D), BF16),
+            pltpu.VMEM((4, 40, TILE), F32),
+            pltpu.VMEM((4, 4, 16, TILE), BF16),
+            pltpu.VMEM((4, 4, 16, TILE), BF16),
+            pltpu.VMEM((2, 4, 16, D), BF16),
+            pltpu.VMEM((2, 4, 16, D), BF16),
+            pltpu.VMEM((4, 16, D), F32),
+            pltpu.VMEM((4, 16, D), BF16),
+            pltpu.VMEM((2, 6, 16, 4 * HD), BF16),
+            pltpu.VMEM((2, 112, 4 * HD), F32),
             dma,
             dma((2, 2, 4)),
             dma,
-            dma((2,)),
-            dma((2, 4)),
-            dma((2, 4)),
+            dma,
+            dma((4,)),
+            dma((4,)),
+            dma((4,)),
+            dma,
+            dma,
             dma((2,)),
             dma((2,)),
-            dma((2,)),
-            dma((2,)),
-            dma,
-            dma((8,)),
-            dma,
-            dma((2,)),
-            dma((2,)),
+            dma,
+            dma,
+            dma,
+            dma,
+            dma,
+            dma,
         ],
         compiler_params=pltpu.CompilerParams(
             collective_id=0, has_side_effects=True, vmem_limit_bytes=60 * 2**20

time: 80 us -> 62.6 us (0.78)
  Pallas kernels: 78.4 us -> 61 us
    pallas_call x1, Pallas kernels: 78.4 us -> 61 us  [shards(): pl.pallas_call(kernel, out_shape=jax.ShapeDtypeStruct((2, 8, D), BF16), i...]
where the time goes in v2:
time: 62.6 us; the launch traced here: 62.5 us
  Pallas kernels  61 us (97%)
  local copies, waits for them, and re-layouts  1.42 us (2%)
    pallas_call x1, Pallas kernels, shards(): pl.pallas_call(kernel, out_shape=jax.ShapeDtypeStruct((2, 8, D), BF16), i...  61 us
    unnamed x1, local copies, waits for them, and re-layouts  1.42 us

profile of v2, /device:TPU:1, one launch (start us, length us, event | category | flops | bytes accessed | tf_op | source)
XLA Modules:
  0.0 62.5 jit_solution(17329702433778565793)
XLA Ops:
  0.0 61.0 %shard_map.118 = bf16[2,8,1536]{2,1,0:T(8,128)(2,1)} custom-call(s32[2]{0:T(128)} %lens.1, bf16[2,128,1536]{2,1,0:T(8,128)(2,1)} %feat.1, f32[2,1536]{1,0:T(2,128)} %gains.1, bf16[3,96,1536]{2,1,0:T(8,128)(2,1)} %wqkv.1, bf16[96,1536]{1,0:T(8,128)(2,1)} %wpos.1, f32[2,96]{1,0:T(2,128)} %pbias.1, bf16[96,1536]{1,0:T(8,128)(2,1)} %wout.1, ...), custom_call_target="tpu_custom_call" | custom-call | tf_op jit(solution)/shard_map/pallas_call | solution.py:437
  61.0 1.4 %copy.14 = bf16[2,8,1536]{2,1,0:T(8,128)(2,1)} copy(bf16[2,8,1536]{2,1,0:T(8,128)(2,1)} %shard_map.118) | data formatting | bytes 98304

commit v3 on v2

--- a/solution.py
+++ b/solution.py
@@ -52,7 +52,7 @@
     feat,
     gains,
     wqkv,
-    wpos,
+    wpos_in,
     pbias,
     wout,
     wcin,
@@ -61,7 +61,6 @@
     cshift,
     wcout,
     out,
-    xs,
     normed,
     kv,
     q_content,
@@ -99,6 +98,8 @@
     halo_recv,
     params_send,
     params_recv,
+    wpos,
+    wpos_sem,
 ):
     t = lax.axis_index("tm")
     s = lax.axis_index("tensor")
@@ -136,6 +137,9 @@
     for peer in peers:
         pl.semaphore_signal(barrier, inc=1, device_id=peer, device_id_type=MESH)
 
+    wpos_copy = pltpu.make_async_copy(wpos_in, wpos, wpos_sem)
+    wpos_copy.start()
+
     params[g, 0:31, 0:HD] = dker[...]
     params[g, 31:32, 0:HD] = cscale[...]
     params[g, 32:33, 0:HD] = cshift[...]
@@ -143,10 +147,9 @@
     gain_one = gains[0:1, :]
     for w in range(2):
 
-        @pl.loop(0, 8)
+        @pl.loop(0, 8, unroll=2)
         def _(i, w=w):
             rows = feat[w, pl.ds(pl.multiple_of(i * 16, 16), 16), :].astype(F32)
-            xs[w, pl.ds(i * 2, 2)] = rows.reshape(2, 8, D)
             normed[pl.ds(pl.multiple_of(w * TILE + i * 16, 16), 16), :] = layer_norm(
                 rows, gain_one
             ).astype(BF16)
@@ -158,32 +161,35 @@
     def block(column, offset):
         return (base if column == 0 else other) + (z + offset) % 8
 
-    def part(v, way, d):
-        return kv.at[v] if d < 3 else kv.at[v, pl.ds(HD * way, HD)]
-
-    def ring_send(column, d):
+    def ring_copy(v, way, column, d, h):
+        ref = kv.at[v, pl.ds(HD * h, HD)]
+        return rcopy(
+            ref,
+            ref,
+            kv_send,
+            ring_recv.at[way, column, d, h],
+            z_right if way == 0 else z_left,
+            s,
+        )
+
+    def ring_send(column, d, h):
         for way in range(2):
-            ref = part(block(column, 8 - d if way == 0 else d), way, d)
-            rcopy(
-                ref,
-                ref,
-                kv_send,
-                ring_recv.at[way, column, d],
-                z_right if way == 0 else z_left,
-                s,
-            ).start()
-
-    def ring_wait(column, d):
+            if d < 3 or h == way:
+                ring_copy(block(column, 8 - d if way == 0 else d), way, column, d, h).start()
+
+    def ring_wait(column, d, h):
         for way in range(2):
-            ref = part(block(column, 7 - d if way == 0 else d + 1), way, d)
-            rcopy(
-                ref,
-                ref,
-                kv_send,
-                ring_recv.at[way, column, d],
-                z_right if way == 0 else z_left,
-                s,
-            ).wait_recv()
+            if d < 3 or h == way:
+                v = block(column, 7 - d if way == 0 else d + 1)
+                ring_copy(v, way, column, d, h).wait_recv()
+
+    def ring_step(column, d, h):
+        ring_wait(column, d, h)
+        ring_send(column, d + 1, h)
+
+    def cross_copy(v, h):
+        ref = kv.at[v, pl.ds(HD * h, HD)]
+        return rcopy(ref, ref, kv_send, cross_recv.at[h], t_cross, s)
 
     own_weights = [wout, wcin.at[0], wcin.at[1], wcout]
 
@@ -206,8 +212,9 @@
         bulk_wait(wbuf.at[m, pl.ds(0, 2)], ws_recv.at[m])
         pltpu.make_async_copy(own_weights[m], wbuf.at[m, g], w_local.at[m]).wait()
 
-    ring_send(0, 0)
-    rcopy(kv.at[t], kv.at[t], kv_send, cross_recv, t_cross, s).start()
+    for h in range(2):
+        ring_send(0, 0, h)
+        cross_copy(t, h).start()
     for m in range(4):
         weights_start(m)
     for k in range(1, 4):
@@ -218,6 +225,7 @@
     query = dot_nt(normed[...], wqkv[0])
     q_content[...] = (query + pbias[0:1, :]).astype(BF16)
     q_position[...] = (query + pbias[1:2, :]).astype(BF16)
+    wpos_copy.wait()
     frequency = jnp.exp(
         lax.broadcasted_iota(jnp.int32, (1, HALF), 1).astype(F32)
         * (-2.0 * math.log(10000.0) / D)
@@ -271,40 +279,48 @@
         content(block(column, 7 - d))
         content(block(column, d + 1))
 
-    ring_wait(0, 0)
-    ring_send(0, 1)
-    rel_tiles(0, 4)
-    rcopy(kv.at[t_cross], kv.at[t_cross], kv_send, cross_recv, t_cross, s).wait_recv()
-    ring_send(1, 0)
-    rel_tiles(4, 8)
-    ring_wait(0, 1)
-    ring_send(0, 2)
-    rel_tiles(8, 12)
-    ring_wait(1, 0)
-    ring_send(1, 1)
-    rel_tiles(12, 17)
-    ring_wait(0, 2)
-    ring_send(0, 3)
+    tile = 0
+    for column, d, h, count in (
+        (0, 0, 0, 2),
+        (0, 0, 1, 2),
+        (1, -1, 0, 1),
+        (1, -1, 1, 1),
+        (0, 1, 0, 1),
+        (0, 1, 1, 2),
+        (1, 0, 0, 1),
+        (1, 0, 1, 2),
+        (0, 2, 0, 1),
+        (0, 2, 1, 2),
+        (1, 1, 0, 1),
+        (1, 1, 1, 1),
+    ):
+        if d < 0:
+            cross_copy(t_cross, h).wait_recv()
+            ring_send(1, 0, h)
+        else:
+            ring_step(column, d, h)
+        rel_tiles(tile, tile + count)
+        tile += count
     content(t)
     content(t_cross)
     content_pair(0, 0)
     weights_x(0)
-    ring_wait(1, 1)
-    ring_send(1, 2)
     content_pair(1, 0)
+    ring_step(1, 2, 0)
     content_pair(0, 1)
-    ring_wait(1, 2)
-    ring_send(1, 3)
-    ring_wait(0, 3)
+    weights_x(1)
     content_pair(0, 2)
+    ring_step(1, 2, 1)
     content_pair(1, 1)
+    weights_x(2)
+    ring_wait(0, 3, 0)
+    ring_wait(0, 3, 1)
     content(block(0, 4))
-    weights_x(1)
     content_pair(1, 2)
-    ring_wait(1, 3)
+    weights_x(3)
+    ring_wait(1, 3, 0)
+    ring_wait(1, 3, 1)
     content(block(1, 4))
-    weights_x(2)
-    weights_x(3)
 
     peak = jnp.max(scores[...], axis=0)
     peak = jnp.max(peak, axis=-1, keepdims=True)
@@ -351,7 +367,10 @@
     total = dot_nn(hrecv[0, :, :, 0:HD].reshape(64, HD), wbuf[0, 0])
     for k in range(1, 4):
         total = total + dot_nn(hrecv[k, :, :, 0:HD].reshape(64, HD), wbuf[0, k])
-    own_rows = jnp.concatenate([xs[0, s], xs[1, s]], axis=0)
+    pairs = [feat[w, pl.ds(pl.multiple_of((s // 2) * 16, 16), 16), :].astype(F32) for w in range(2)]
+    own_rows = jnp.concatenate(
+        [jnp.where(core == 0, pair[0:8], pair[8:16]) for pair in pairs], axis=0
+    )
     hidden = (own_rows + reduce_rows(0, total)).astype(BF16).astype(F32)
     nbuf[y] = layer_norm(hidden, gains[1:2, :]).astype(BF16)
 
@@ -433,14 +452,14 @@
     conv_out_weight,
 ):
     vmem = pl.BlockSpec(memory_space=pltpu.VMEM)
+    hbm = pl.BlockSpec(memory_space=pl.ANY)
     dma = pltpu.SemaphoreType.DMA
     return pl.pallas_call(
         kernel,
         out_shape=jax.ShapeDtypeStruct((2, 8, D), BF16),
-        in_specs=[pl.BlockSpec(memory_space=pltpu.SMEM)] + [vmem] * 11,
+        in_specs=[pl.BlockSpec(memory_space=pltpu.SMEM)] + [vmem] * 3 + [hbm, vmem, hbm, hbm] + [vmem] * 3 + [hbm],
         out_specs=vmem,
         scratch_shapes=[
-            pltpu.VMEM((2, 16, 8, D), F32),
             pltpu.VMEM((256, D), BF16),
             pltpu.VMEM((16, 2 * HD, 256), BF16),
             pltpu.VMEM((256, HD), BF16),
@@ -462,8 +481,8 @@
             pltpu.VMEM((2, 6, 16, 4 * HD), BF16),
             pltpu.VMEM((2, 112, 4 * HD), F32),
             dma,
-            dma((2, 2, 4)),
-            dma,
+            dma((2, 2, 4, 2)),
+            dma((2,)),
             dma,
             dma((4,)),
             dma((4,)),
@@ -477,6 +496,8 @@
             dma,
             dma,
             dma,
+            dma,
+            pltpu.VMEM((HD, D), BF16),
             dma,
         ],
         compiler_params=pltpu.CompilerParams(

time: 62.6 us -> 60.9 us (0.973)
  Pallas kernels: 61 us -> 59.3 us
    pallas_call x1, Pallas kernels: 61 us -> 59.3 us  [shards(): pl.pallas_call(kernel, out_shape=jax.ShapeDtypeStruct((2, 8, D), BF16), i...]
where the time goes in v3:
time: 60.9 us; the launch traced here: 60.7 us
  Pallas kernels  59.3 us (97%)
  local copies, waits for them, and re-layouts  1.42 us (2%)
    pallas_call x1, Pallas kernels, shards(): pl.pallas_call(kernel, out_shape=jax.ShapeDtypeStruct((2, 8, D), BF16), i...  59.3 us
    unnamed x1, local copies, waits for them, and re-layouts  1.42 us

profile of v3, /device:TPU:1, one launch (start us, length us, event | category | flops | bytes accessed | tf_op | source)
XLA Modules:
  0.0 60.7 jit_solution(2857365541102870119)
XLA Ops:
  0.0 59.3 %shard_map.118 = bf16[2,8,1536]{2,1,0:T(8,128)(2,1)} custom-call(s32[2]{0:T(128)} %lens.1, bf16[2,128,1536]{2,1,0:T(8,128)(2,1)} %feat.1, f32[2,1536]{1,0:T(2,128)} %gains.1, bf16[3,96,1536]{2,1,0:T(8,128)(2,1)} %wqkv.1, bf16[96,1536]{1,0:T(8,128)(2,1)} %wpos_in.1, f32[2,96]{1,0:T(2,128)} %pbias.1, bf16[96,1536]{1,0:T(8,128)(2,1)} %wout.1, ...), custom_call_target="tpu_custom_call" | custom-call | tf_op jit(solution)/shard_map/pallas_call | solution.py:457
  59.3 1.4 %copy.14 = bf16[2,8,1536]{2,1,0:T(8,128)(2,1)} copy(bf16[2,8,1536]{2,1,0:T(8,128)(2,1)} %shard_map.118) | data formatting | bytes 98304

commit v4 on v3

--- a/solution.py
+++ b/solution.py
@@ -100,6 +100,7 @@
     params_recv,
     wpos,
     wpos_sem,
+    relay,
 ):
     t = lax.axis_index("tm")
     s = lax.axis_index("tensor")
@@ -352,12 +353,23 @@
     def reduce_rows(i, total):
         total = total.reshape(4, 16, D)
         psend[i] = total.astype(BF16)
-        for k in (2, 1, 3):
-            rcopy(
-                psend.at[i, (y + k) % 4], precv.at[i, y], p_send.at[i], p_recv.at[i], t, y_peer(k)
-            ).start()
+        def hop(src, dst, sem, k):
+            return rcopy(src, dst, p_send.at[i], p_recv.at[i, sem], t, y_peer(k))
+
+        left, right, far = (y + 3) % 4, (y + 1) % 4, (y + 2) % 4
+        halves = [pl.ds(0, HALF), pl.ds(HALF, HALF)]
+        for h, k in ((0, 1), (1, 3)):
+            hop(psend.at[i, far, :, halves[h]], relay.at[i, h], h, k).start()
+        hop(psend.at[i, right], precv.at[i, y], 2, 1).start()
+        hop(psend.at[i, left], precv.at[i, y], 3, 3).start()
         pown[...] = total
-        bulk_wait(precv.at[i, pl.ds(0, 3)], p_recv.at[i])
+        for h, k, origin in ((0, 1, left), (1, 3, right)):
+            bulk_wait(relay.at[i, h], p_recv.at[i, h])
+            hop(relay.at[i, h], precv.at[i, origin, :, halves[h]], 4 + h, k).start()
+        bulk_wait(precv.at[i, left], p_recv.at[i, 2])
+        bulk_wait(precv.at[i, right], p_recv.at[i, 3])
+        for h in range(2):
+            bulk_wait(precv.at[i, far, :, halves[h]], p_recv.at[i, 4 + h])
         result = pown[y]
         for k in range(1, 4):
             result = result + precv[i, (y + k) % 4].astype(F32)
@@ -374,11 +386,25 @@
     hidden = (own_rows + reduce_rows(0, total)).astype(BF16).astype(F32)
     nbuf[y] = layer_norm(hidden, gains[1:2, :]).astype(BF16)
 
-    for k in (2, 1, 3):
-        rcopy(nbuf.at[y], nbuf.at[y], n_send, n_recv, t, y_peer(k)).start()
+    def n_copy(p, h, sem, k):
+        ref = nbuf.at[p, :, pl.ds(HALF * h, HALF)]
+        return rcopy(ref, ref, n_send, n_recv.at[sem], t, y_peer(k))
+
+    left, right, far = (y + 3) % 4, (y + 1) % 4, (y + 2) % 4
+    n_copy(y, 0, 0, 1).start()
+    n_copy(y, 1, 3, 3).start()
+    n_copy(y, 1, 1, 1).start()
+    n_copy(y, 0, 2, 3).start()
+    n_copy(left, 0, 0, 1).wait_recv()
+    n_copy(left, 0, 4, 1).start()
+    n_copy(right, 1, 3, 3).wait_recv()
+    n_copy(right, 1, 5, 3).start()
     weights_end(1)
     weights_end(2)
-    bulk_wait(nbuf.at[pl.ds(0, 3)], n_recv)
+    n_copy(left, 1, 1, 1).wait_recv()
+    n_copy(right, 0, 2, 3).wait_recv()
+    n_copy(far, 0, 4, 1).wait_recv()
+    n_copy(far, 1, 5, 3).wait_recv()
 
     rows_all = nbuf[...].reshape(64, D)
     opened = dot_nt(rows_all, wbuf[1].reshape(4 * HD, D))
@@ -432,7 +458,7 @@
     bulk_wait(params.at[pl.ds(0, 3)], params_send)
     bulk_wait(hsend.at[pl.ds(0, 3)], a2a_send)
     for i in range(2):
-        bulk_wait(psend.at[i, pl.ds(0, 3)], p_send.at[i])
+        bulk_wait(psend.at[i], p_send.at[i])
     bulk_wait(nbuf.at[pl.ds(0, 3)], n_send)
     bulk_wait(gx.at[:, pl.ds(0, 4)], halo_send)
 
@@ -490,15 +516,16 @@
             dma,
             dma,
             dma((2,)),
-            dma((2,)),
-            dma,
-            dma,
+            dma((2, 6)),
+            dma,
+            dma((6,)),
             dma,
             dma,
             dma,
             dma,
             pltpu.VMEM((HD, D), BF16),
             dma,
+            pltpu.VMEM((2, 2, 16, HALF), BF16),
         ],
         compiler_params=pltpu.CompilerParams(
             collective_id=0, has_side_effects=True, vmem_limit_bytes=60 * 2**20

time: 60.9 us -> 66.7 us (1.095)
  Pallas kernels: 59.3 us -> 64.5 us
    pallas_call x1, Pallas kernels: 59.3 us -> 64.5 us  [shards(): pl.pallas_call(kernel, out_shape=jax.ShapeDtypeStruct((2, 8, D), BF16), i...]
where the time goes in v4:
time: 66.7 us; the launch traced here: 65.9 us
  Pallas kernels  64.5 us (97%)
  local copies, waits for them, and re-layouts  1.42 us (2%)
    pallas_call x1, Pallas kernels, shards(): pl.pallas_call(kernel, out_shape=jax.ShapeDtypeStruct((2, 8, D), BF16), i...  64.5 us
    unnamed x1, local copies, waits for them, and re-layouts  1.42 us

profile of v4, /device:TPU:1, one launch (start us, length us, event | category | flops | bytes accessed | tf_op | source)
XLA Modules:
  0.0 65.9 jit_solution(1298693371384785312)
XLA Ops:
  0.0 64.5 %shard_map.118 = bf16[2,8,1536]{2,1,0:T(8,128)(2,1)} custom-call(s32[2]{0:T(128)} %lens.1, bf16[2,128,1536]{2,1,0:T(8,128)(2,1)} %feat.1, f32[2,1536]{1,0:T(2,128)} %gains.1, bf16[3,96,1536]{2,1,0:T(8,128)(2,1)} %wqkv.1, bf16[96,1536]{1,0:T(8,128)(2,1)} %wpos_in.1, f32[2,96]{1,0:T(2,128)} %pbias.1, bf16[96,1536]{1,0:T(8,128)(2,1)} %wout.1, ...), custom_call_target="tpu_custom_call" | custom-call | tf_op jit(solution)/shard_map/pallas_call | solution.py:483
  64.5 1.4 %copy.14 = bf16[2,8,1536]{2,1,0:T(8,128)(2,1)} copy(bf16[2,8,1536]{2,1,0:T(8,128)(2,1)} %shard_map.118) | data formatting | bytes 98304

commit v5 on v3

--- a/solution.py
+++ b/solution.py
@@ -147,7 +147,7 @@
     gain_one = gains[0:1, :]
     for w in range(2):
 
-        @pl.loop(0, 8, unroll=2)
+        @pl.loop(0, 8, unroll=4)
         def _(i, w=w):
             rows = feat[w, pl.ds(pl.multiple_of(i * 16, 16), 16), :].astype(F32)
             normed[pl.ds(pl.multiple_of(w * TILE + i * 16, 16), 16), :] = layer_norm(

time: 60.9 us -> 60.5 us (level)
  no operation moved by 1% of the time
where the time goes in v5:
time: 60.5 us; the launch traced here: 60.4 us
  Pallas kernels  59 us (98%)
  local copies, waits for them, and re-layouts  1.42 us (2%)
    pallas_call x1, Pallas kernels, shards(): pl.pallas_call(kernel, out_shape=jax.ShapeDtypeStruct((2, 8, D), BF16), i...  59 us
    unnamed x1, local copies, waits for them, and re-layouts  1.42 us

profile of v5, /device:TPU:1, one launch (start us, length us, event | category | flops | bytes accessed | tf_op | source)
XLA Modules:
  0.0 60.4 jit_solution(14832456589727396023)
XLA Ops:
  0.0 59.0 %shard_map.118 = bf16[2,8,1536]{2,1,0:T(8,128)(2,1)} custom-call(s32[2]{0:T(128)} %lens.1, bf16[2,128,1536]{2,1,0:T(8,128)(2,1)} %feat.1, f32[2,1536]{1,0:T(2,128)} %gains.1, bf16[3,96,1536]{2,1,0:T(8,128)(2,1)} %wqkv.1, bf16[96,1536]{1,0:T(8,128)(2,1)} %wpos_in.1, f32[2,96]{1,0:T(2,128)} %pbias.1, bf16[96,1536]{1,0:T(8,128)(2,1)} %wout.1, ...), custom_call_target="tpu_custom_call" | custom-call | tf_op jit(solution)/shard_map/pallas_call | solution.py:457
  59.0 1.4 %copy.14 = bf16[2,8,1536]{2,1,0:T(8,128)(2,1)} copy(bf16[2,8,1536]{2,1,0:T(8,128)(2,1)} %shard_map.118) | data formatting | bytes 98304
